TPU v7x, 32 devices: a whole 2x2x4 slice. The times are simulated.
32 devices in a mesh: wide: 4 (over x, core), narrow: 8 (over z, y).
Axes of the slice: x: 2, y: 2, z: 4, core: 2. Of those that a mesh axis runs over, the one named last changes fastest.
Arguments:
- grad_parts: bfloat16 [4, 3584, 8192], P('wide', 'narrow'), may hold values from -6 to 6
- master: bfloat16 [3584, 8192], P('narrow'), may hold values from -0.1875 to 0.1875
- moment_one: float32 [3584, 8192], P('narrow'), may hold values from -4 to 4
- moment_two: float32 [3584, 8192], P('narrow'), may hold values from 0.01 to 1
- gate_up: bfloat16 [3584, 2, 8192], P(None, None, 'narrow'), may hold values from -0.09375 to 0.09375
- tokens: bfloat16 [64, 3584], P(('wide', 'narrow')), may hold values from -6 to 6
- expert_ids: int32 [64, 4], P(('wide', 'narrow')), may hold values from 0 to 7, all different within a row; in each aligned block of 2 rows (0 to 1, 2 to 3, ...) at most 2 rows name the same one
- gate_vals: bfloat16 [64, 4], P(('wide', 'narrow')), may hold values from 0.049804688 to 1
Outputs:
- new_master: bfloat16 [3584, 8192], P('narrow')
- new_one: float32 [3584, 8192], P('narrow')
- new_two: float32 [3584, 8192], P('narrow')
- combined: bfloat16 [64, 3584], P(('wide', 'narrow'))
Inputs may be any that keep to these rules, and one draw needn't show every extreme that they name: `expert_ids`: each token names 4 distinct experts; each device's 2 tokens name every expert at most 2 times (which follows from the distinct ids), and some device names one expert twice.
All inputs are finite; a program needn't handle non-finite values.
Results may differ from a plain program's by a relative error of at most 0.022.
Values may be sent and summed in bfloat16 or wider, within the bound.
No kernel may reach another device: no remote copies, remote signals or barrier semaphores. Data moves between devices by JAX's collectives and lax.ppermute only.
A program may use at most 192 MiB of HBM per device.

v0:
```python
import jax
import jax.numpy as jnp
from jax import lax
from jax.sharding import PartitionSpec as P

EXPERTS = 8
TOPK = 4
QBLOCK = 128
CAP = 2
beta_first = 0.9
beta_second = 0.95
learn_rate = 0.003
adam_eps = 1e-08
quant_limit = 448.0
amax_eps = 1e-06
bias_first = 1.0 - 0.9**10
bias_second = 1.0 - 0.95**10


def adam_quant(grad_sum, master, moment_one, moment_two):
    new_one = beta_first * moment_one + (1.0 - beta_first) * grad_sum
    new_two = beta_second * moment_two + (1.0 - beta_second) * grad_sum * grad_sum
    step_dir = new_one / bias_first / (jnp.sqrt(new_two / bias_second) + adam_eps)
    updated = master.astype(jnp.float32) - learn_rate * step_dir
    row_count, col_count = updated.shape
    blocks = updated.reshape(row_count, col_count // QBLOCK, QBLOCK)
    scales = ((jnp.max(jnp.abs(blocks), axis=2) + amax_eps) / quant_limit).astype(jnp.bfloat16)
    quanta = (
        (blocks / scales.astype(jnp.float32)[:, :, None])
        .astype(jnp.bfloat16)
        .reshape(row_count, col_count)
    )
    return (updated.astype(jnp.bfloat16), new_one, new_two, quanta, scales)


def expert_rows(rows_in, gate_piece, quanta, scales):
    unit_count = gate_piece.shape[2]
    proj_both = jnp.dot(
        rows_in,
        gate_piece.reshape(gate_piece.shape[0], 2 * unit_count),
        preferred_element_type=jnp.float32,
    )
    hidden = (jax.nn.silu(proj_both[:, :unit_count]) * proj_both[:, unit_count:]).astype(
        jnp.bfloat16
    )
    block_count = unit_count // QBLOCK
    per_block = jnp.einsum(
        "rbf,dbf->rbd",
        hidden.reshape(-1, block_count, QBLOCK),
        quanta.reshape(quanta.shape[0], block_count, QBLOCK),
        preferred_element_type=jnp.float32,
    )
    return jnp.einsum("rbd,db->rd", per_block, scales.astype(jnp.float32))


def body(grad_parts, master, moment_one, moment_two, gate_up, tokens, expert_ids, gate_vals):
    grad_sum = lax.psum(grad_parts[0], "wide").astype(jnp.float32)
    new_master, new_one, new_two, quanta, scales = adam_quant(
        grad_sum, master, moment_one, moment_two
    )
    owned_q, owned_s = (
        lax.all_to_all(quanta, "narrow", split_axis=1, concat_axis=0, tiled=True),
        lax.all_to_all(scales, "narrow", split_axis=1, concat_axis=0, tiled=True),
    )
    onehot = (expert_ids[:, :, None] == jnp.arange(EXPERTS, dtype=jnp.int32)[None, None, :]).astype(
        jnp.float32
    )
    gate_float = gate_vals.astype(jnp.float32)
    group_size = lax.axis_size("narrow") // EXPERTS
    tok_count = tokens.shape[0]
    feat_width = tokens.shape[1]
    flat_ids = onehot.reshape(-1, EXPERTS)
    assign_count = flat_ids.shape[0]
    earlier = (jnp.arange(assign_count)[:, None] > jnp.arange(assign_count)[None, :]).astype(
        jnp.float32
    )
    slot_rank = jnp.sum(jnp.dot(earlier, flat_ids) * flat_ids, axis=1)
    slot_hit = (slot_rank[:, None] == jnp.arange(CAP)[None, :].astype(jnp.float32)).astype(
        jnp.float32
    )
    tok_sel = (jnp.arange(assign_count)[:, None] // TOPK == jnp.arange(tok_count)[None, :]).astype(
        jnp.float32
    )
    dispatch_map = jnp.einsum("ae,ac,at->ect", flat_ids, slot_hit, tok_sel)
    combine_weight = jnp.einsum(
        "ae,ac,at->ect", flat_ids * gate_float.reshape(-1)[:, None], slot_hit, tok_sel
    )
    slot_rows = jnp.einsum(
        "ect,td->ecd", dispatch_map.astype(jnp.bfloat16), tokens, preferred_element_type=jnp.float32
    ).astype(jnp.bfloat16)
    outgoing = jnp.repeat(slot_rows, group_size, axis=0)
    received = lax.all_to_all(outgoing, "narrow", split_axis=0, concat_axis=0, tiled=True)
    src_count, slot_count, width_in = received.shape
    partial_value = expert_rows(
        received.reshape(src_count * slot_count, width_in), gate_up, owned_q, owned_s
    )
    partial_value = partial_value.astype(jnp.bfloat16).reshape(src_count, slot_count, width_in)
    returned = lax.all_to_all(partial_value, "narrow", split_axis=0, concat_axis=0, tiled=True)
    summed = jnp.sum(
        returned.astype(jnp.float32).reshape(EXPERTS, group_size, CAP, feat_width), axis=1
    )
    combined = jnp.einsum("ect,ecd->td", combine_weight, summed)
    return (new_master, new_one, new_two, combined.astype(jnp.bfloat16))


def solution(mesh):
    in_specs = (
        P("wide", "narrow", None),
        P("narrow", None),
        P("narrow", None),
        P("narrow", None),
        P(None, None, "narrow"),
        P(("wide", "narrow"), None),
        P(("wide", "narrow"), None),
        P(("wide", "narrow"), None),
    )
    out_specs = (
        P("narrow", None),
        P("narrow", None),
        P("narrow", None),
        P(("wide", "narrow"), None),
    )
    return jax.shard_map(body, mesh=mesh, in_specs=in_specs, out_specs=out_specs, check_vma=False)
```

profile of v0, /device:TPU:0, one launch (start us, length us, event | category | flops | bytes accessed | tf_op | source)
XLA Modules:
  0.0 432.0 jit_solution(17425737134282565379)
XLA Ops:
  7.2 0.7 all-reduce.2.cloned.1.call-update
  7.9 0.8 eq.46
  8.9 0.3 convolution_convert_fusion
  9.2 0.7 copy.32
  10.0 7.3 %all-to-all-start.2 = ((bf16[8,2,3584]{2,1,0:T(2,128)(2,1)}), bf16[8,2,3584]{2,1,0:T(2,128)(2,1)S(1)}, u32[]{:S(2)}, u32[]{:S(2)}) async-start(bf16[8,2,3584]{2,1,0:T(2,128)(2,1)} %copy.32), calls=%async_computation.2 | async-start | bytes 229376 | tf_op jit(solution)/shard_map/all_to_all | solution.py:92
  17.3 132.4 %all-reduce.2.cloned.1.call-done = bf16[448,8192]{1,0:T(8,128)(2,1)} async-done(((bf16[448,8192]{1,0:T(8,128)(2,1)}), bf16[448,8192]{1,0:T(8,128)(2,1)}) %all-reduce.2.cloned.1.call-update) | async-done | bytes 7340048 | tf_op jit(solution)/shard_map/psum | solution.py:57
  149.7 34.3 %abs_bitcast_fusion = (f32[56,8,64,128]{3,1,2,0:T(8,128)}, f32[448,8192]{1,0:T(8,128)}, f32[448,8192]{1,0:T(8,128)}, f32[448,8192]{1,0:T(8,128)}) fusion(bf16[448,8192]{1,0:T(8,128)(2,1)} %param.9, bf16[448,8192]{1,0:T(8,128)(2,1)} %all-reduce.2.cloned.1.call-done, f32[448,8192]{1,0:T(8,128)} %param.10, f32[448,8192]{1,0:T(8,128)} %param.11), kind=kLoop, calls=%fused_computation.6 | loop fusion | flops 58720256 | bytes 102760448
  184.0 13.6 %copy.49 = f32[56,8,64,128]{3,2,1,0:T(8,128)} copy(f32[56,8,64,128]{3,1,2,0:T(8,128)} %get-tuple-element.4) | data formatting | bytes 29360128
  197.6 9.0 %reduce_max.9 = f32[448,64]{1,0:T(8,128)S(1)} reduce(f32[448,64,128]{2,1,0:T(8,128)} %bitcast.68, f32[]{:T(128)} %constant.46.clone.1), dimensions={2}, to_apply=%region_2.0 | reduce | flops 3641344 | bytes 14794756 | tf_op jit(solution)/shard_map/reduce_max | solution.py:27
  206.8 0.6 fusion.23
  207.6 5.5 %all-to-all-start = ((bf16[448,8,8]{0,2,1:T(8,128)(2,1)}), bf16[448,8,8]{0,2,1:T(8,128)(2,1)S(1)}, u32[]{:S(2)}, u32[]{:S(2)}) async-start(bf16[448,8,8]{0,2,1:T(8,128)(2,1)} %get-tuple-element.10), calls=%async_computation | async-start | bytes 131072 | tf_op jit(solution)/shard_map/all_to_all | solution.py:63
  213.1 4.0 div.53
  217.2 18.6 %fusion.2 = (bf16[448,8192]{1,0:T(8,128)(2,1)S(1)}, bf16[448,8192]{1,0:T(8,128)(2,1)}) fusion(f32[448,8192]{1,0:T(8,128)} %get-tuple-element.5, f32[56,8,64,128]{3,2,1,0:T(8,128)S(1)} %bitcast.69), kind=kLoop, calls=%fused_computation.5 | loop fusion | flops 11010048 | bytes 44040192 | tf_op jit(solution)/shard_map/convert_element_type | solution.py:30
  235.7 4.1 copy.69
  239.9 6.0 %all-to-all-start.1 = ((bf16[448,8,1024]{2,0,1:T(8,128)(2,1)}), bf16[448,8,1024]{2,0,1:T(8,128)(2,1)}, u32[]{:S(2)}, u32[]{:S(2)}) async-start(bf16[448,8,1024]{2,0,1:T(8,128)(2,1)} %bitcast.70), calls=%async_computation.1 | async-start | bytes 14680064 | tf_op jit(solution)/shard_map/all_to_all | solution.py:62
  245.9 16.1 %copy.52 = bf16[448,8,2,1024]{3,1,2,0:T(8,128)(2,1)} copy(bf16[448,8,2,1024]{3,2,1,0:T(2,128)(2,1)} %bitcast.72) | data formatting | bytes 29360128
  262.0 7.2 %fusion.57 = f32[16,2048]{1,0:T(8,128)S(1)} fusion(bf16[16,3584]{1,0:T(8,128)(2,1)S(1)} %reshape.99, bf16[3584,2048]{1,0:T(8,128)(2,1)} %bitcast.67), kind=kOutput, calls=%fused_computation.57 | convolution fusion | flops 234881024 | bytes 14925824 | tf_op jit(solution)/shard_map/dot_general | solution.py:38
  269.3 136.2 %all-to-all-done.1 = bf16[448,8,1024]{2,0,1:T(8,128)(2,1)} async-done(((bf16[448,8,1024]{2,0,1:T(8,128)(2,1)}), bf16[448,8,1024]{2,0,1:T(8,128)(2,1)}, u32[]{:S(2)}, u32[]{:S(2)}) %all-to-all-start.1) | async-done | bytes 7340064 | tf_op jit(solution)/shard_map/all_to_all | solution.py:62
  405.6 5.0 %copy.51 = bf16[448,8,8,128]{3,2,1,0:T(8,128)(2,1)S(1)} copy(bf16[448,8,8,128]{3,1,2,0:T(8,128)(2,1)} %bitcast.24) | data formatting | bytes 14680064
  410.5 2.1 fusion.12
  412.6 0.7 reshape.102
  413.3 3.6 all-to-all-start.3
  417.0 7.1 %all-to-all-done.3 = bf16[8,2,3584]{2,1,0:T(2,128)(2,1)S(1)} async-done(((bf16[8,2,3584]{2,1,0:T(2,128)(2,1)}), bf16[8,2,3584]{2,1,0:T(2,128)(2,1)S(1)}, u32[]{:S(2)}, u32[]{:S(2)}) %all-to-all-start.3) | async-done | bytes 114720 | tf_op jit(solution)/shard_map/all_to_all | solution.py:98
  424.2 0.9 fusion.11
  (20 shorter events, 0.8 us)
Async XLA Ops:
  7.2 1.7 copy-start
  7.2 142.6 %all-reduce.2.cloned.1.call-start = ((), (), s32[]{:S(2)}) async-start(), calls=%async_computation.4 | async-start | bytes 14680064 | tf_op jit(solution)/shard_map/psum | solution.py:57
  10.0 197.6 %all-to-all-start.2 = ((bf16[8,2,3584]{2,1,0:T(2,128)(2,1)}), bf16[8,2,3584]{2,1,0:T(2,128)(2,1)S(1)}, u32[]{:S(2)}, u32[]{:S(2)}) async-start(bf16[8,2,3584]{2,1,0:T(2,128)(2,1)} %copy.32), calls=%async_computation.2 | async-start | bytes 229376 | tf_op jit(solution)/shard_map/all_to_all | solution.py:92
  207.6 32.3 %all-to-all-start = ((bf16[448,8,8]{0,2,1:T(8,128)(2,1)}), bf16[448,8,8]{0,2,1:T(8,128)(2,1)S(1)}, u32[]{:S(2)}, u32[]{:S(2)}) async-start(bf16[448,8,8]{0,2,1:T(8,128)(2,1)} %get-tuple-element.10), calls=%async_computation | async-start | bytes 131072 | tf_op jit(solution)/shard_map/all_to_all | solution.py:63
  239.9 165.7 %all-to-all-start.1 = ((bf16[448,8,1024]{2,0,1:T(8,128)(2,1)}), bf16[448,8,1024]{2,0,1:T(8,128)(2,1)}, u32[]{:S(2)}, u32[]{:S(2)}) async-start(bf16[448,8,1024]{2,0,1:T(8,128)(2,1)} %bitcast.70), calls=%async_computation.1 | async-start | bytes 14680064 | tf_op jit(solution)/shard_map/all_to_all | solution.py:62
  262.0 163.1 %copy-start.1 = (bf16[2,3584]{1,0:T(2,128)(2,1)S(1)}, bf16[2,3584]{1,0:T(2,128)(2,1)}, u32[]{:S(2)}) copy-start(bf16[2,3584]{1,0:T(2,128)(2,1)} %param.13) | copy-start | bytes 43012
  269.2 147.8 %copy-start.2 = (bf16[2,4]{1,0:T(2,128)(2,1)S(1)}, bf16[2,4]{1,0:T(2,128)(2,1)}, u32[]{:S(2)}) copy-start(bf16[2,4]{1,0:T(2,128)(2,1)} %param.15) | copy-start | bytes 52
  413.3 10.9 %all-to-all-start.3 = ((bf16[8,2,3584]{2,1,0:T(2,128)(2,1)}), bf16[8,2,3584]{2,1,0:T(2,128)(2,1)S(1)}, u32[]{:S(2)}, u32[]{:S(2)}) async-start(bf16[8,2,3584]{2,1,0:T(2,128)(2,1)} %reshape.102), calls=%async_computation.3 | async-start | bytes 229376 | tf_op jit(solution)/shard_map/all_to_all | solution.py:98
Sparse Core Ops, SparseCore 0:
  10.4 139.3 all-reduce.1
where the time goes:
time: 433 us; the launch traced here: 432 us
  waiting for transfers between devices  276 us (64%)
  other arithmetic  62.6 us (14%)
  local copies, waits for them, and re-layouts  45.6 us (11%)
  starting transfers between devices  22.5 us (5%)
  between operations  14.1 us (3%)
  matrix products  10.7 us (2%)
    all_to_all x1, waiting for transfers between devices, body(): lax.all_to_all(quanta, 'narrow', split_axis=1, concat_axis=0, tiled=True)  136 us
    psum x1, waiting for transfers between devices, body(): grad_sum = lax.psum(grad_parts[0], 'wide').astype(jnp.float32)  132 us
    unnamed x9, local copies, waits for them, and re-layouts  34.7 us
    unnamed x2, other arithmetic  34.3 us
    convert_element_type x1, other arithmetic, adam_quant(): quanta = (blocks / scales.astype(jnp.float32)[:, :, None]).astype(jnp.bfl...  18.6 us
    reduce_max x1, other arithmetic, adam_quant(): jnp.max(jnp.abs(blocks), axis=2) + amax_eps  9.03 us
  transfers between devices with their start and end apart: 5, of which 3 were waited for; matrix products, arithmetic and copies ran while one was open for 25% of the time, Pallas kernels for 0%

commit v1 on v0

--- a/solution.py
+++ b/solution.py
@@ -54,7 +54,10 @@
 
 
 def body(grad_parts, master, moment_one, moment_two, gate_up, tokens, expert_ids, gate_vals):
-    grad_sum = lax.psum(grad_parts[0], "wide").astype(jnp.float32)
+    _treat_windows = lambda x_in, dev_axis: jnp.sum(
+        lax.all_gather(x_in, axis_name=dev_axis), axis=0
+    )
+    grad_sum = _treat_windows(grad_parts[0], "wide").astype(jnp.float32)
     new_master, new_one, new_two, quanta, scales = adam_quant(
         grad_sum, master, moment_one, moment_two
     )

time: 433 us -> 489 us (1.13)
  waiting for transfers between devices: 276 us -> 318 us
  other arithmetic: 62.6 us -> 77.3 us
    all_gather x0 -> x1, waiting for transfers between devices: none -> 173 us  [body(): lax.all_gather(x_in, axis_name=dev_axis)]
    psum x1 -> x0, waiting for transfers between devices: 132 us -> none  [body(): grad_sum = lax.psum(grad_parts[0], 'wide').astype(jnp.float32)]
    reduce_sum x0 -> x1, other arithmetic: none -> 14.7 us  [body(): jnp.sum(lax.all_gather(x_in, axis_name=dev_axis), axis=0)]
  transfers between devices with their start and end apart: 5 -> 5, of which waited for: 3 -> 3; matrix products, arithmetic and copies ran while one was open for 25% -> 26% of each run, Pallas kernels for 0% -> 0%
where the time goes in v1:
time: 489 us; the launch traced here: 488 us
  waiting for transfers between devices  318 us (65%)
  other arithmetic  77.3 us (16%)
  local copies, waits for them, and re-layouts  45.6 us (9%)
  starting transfers between devices  22.5 us (5%)
  between operations  14.1 us (3%)
  matrix products  10.7 us (2%)
    all_gather x1, waiting for transfers between devices, body(): lax.all_gather(x_in, axis_name=dev_axis)  173 us
    all_to_all x1, waiting for transfers between devices, body(): lax.all_to_all(quanta, 'narrow', split_axis=1, concat_axis=0, tiled=True)  137 us
    unnamed x9, local copies, waits for them, and re-layouts  34.7 us
    unnamed x2, other arithmetic  34.3 us
    convert_element_type x1, other arithmetic, adam_quant(): quanta = (blocks / scales.astype(jnp.float32)[:, :, None]).astype(jnp.bfl...  18.6 us
    reduce_sum x1, other arithmetic, body(): jnp.sum(lax.all_gather(x_in, axis_name=dev_axis), axis=0)  14.7 us
  transfers between devices with their start and end apart: 5, of which 3 were waited for; matrix products, arithmetic and copies ran while one was open for 26% of the time, Pallas kernels for 0%

profile of v1, /device:TPU:0, one launch (start us, length us, event | category | flops | bytes accessed | tf_op | source)
XLA Modules:
  0.0 488.1 jit_solution(4888091112879184035)
XLA Ops:
  7.2 0.7 all-gather.2.cloned.1.call-update
  7.9 0.8 eq.46
  9.2 0.7 copy.32
  10.0 7.3 %all-to-all-start.2 = ((bf16[8,2,3584]{2,1,0:T(2,128)(2,1)}), bf16[8,2,3584]{2,1,0:T(2,128)(2,1)S(1)}, u32[]{:S(2)}, u32[]{:S(2)}) async-start(bf16[8,2,3584]{2,1,0:T(2,128)(2,1)} %copy.32), calls=%async_computation.2 | async-start | bytes 229376 | tf_op jit(solution)/shard_map/all_to_all | solution.py:95
  17.3 173.0 %all-gather.2.cloned.1.call-done = bf16[4,448,8192]{2,1,0:T(8,128)(2,1)} async-done(((bf16[1,448,8192]{2,1,0:T(8,128)(2,1)}), bf16[4,448,8192]{2,1,0:T(8,128)(2,1)}) %all-gather.2.cloned.1.call-update) | async-done | bytes 29360144 | tf_op jit(solution)/shard_map/all_gather | solution.py:58
  190.3 14.7 %reduce_sum.25 = bf16[448,8192]{1,0:T(8,128)(2,1)} reduce(bf16[4,448,8192]{2,1,0:T(8,128)(2,1)} %all-gather.2.cloned.1.call-done, bf16[]{:T(256)} %constant.34.clone.1), dimensions={0}, to_apply=%region_0.0 | reduce | flops 11010048 | bytes 36700160 | tf_op jit(solution)/shard_map/reduce_sum | solution.py:57
  205.0 34.3 %abs_bitcast_fusion = (f32[56,8,64,128]{3,1,2,0:T(8,128)}, f32[448,8192]{1,0:T(8,128)}, f32[448,8192]{1,0:T(8,128)}, f32[448,8192]{1,0:T(8,128)}) fusion(bf16[448,8192]{1,0:T(8,128)(2,1)} %param.9, bf16[448,8192]{1,0:T(8,128)(2,1)} %reduce_sum.25, f32[448,8192]{1,0:T(8,128)} %param.10, f32[448,8192]{1,0:T(8,128)} %param.11), kind=kLoop, calls=%fused_computation.6 | loop fusion | flops 58720256 | bytes 102760448
  239.3 13.6 %copy.49 = f32[56,8,64,128]{3,2,1,0:T(8,128)} copy(f32[56,8,64,128]{3,1,2,0:T(8,128)} %get-tuple-element.4) | data formatting | bytes 29360128
  252.9 9.0 %reduce_max.9 = f32[448,64]{1,0:T(8,128)S(1)} reduce(f32[448,64,128]{2,1,0:T(8,128)} %bitcast.67, f32[]{:T(128)} %constant.48.clone.1), dimensions={2}, to_apply=%region_2.0 | reduce | flops 3641344 | bytes 14794756 | tf_op jit(solution)/shard_map/reduce_max | solution.py:27
  262.1 0.6 fusion.23
  262.9 5.5 %all-to-all-start = ((bf16[448,8,8]{0,2,1:T(8,128)(2,1)}), bf16[448,8,8]{0,2,1:T(8,128)(2,1)S(1)}, u32[]{:S(2)}, u32[]{:S(2)}) async-start(bf16[448,8,8]{0,2,1:T(8,128)(2,1)} %get-tuple-element.10), calls=%async_computation | async-start | bytes 131072 | tf_op jit(solution)/shard_map/all_to_all | solution.py:66
  268.4 4.0 div.53
  272.5 18.6 %fusion.2 = (bf16[448,8192]{1,0:T(8,128)(2,1)S(1)}, bf16[448,8192]{1,0:T(8,128)(2,1)}) fusion(f32[448,8192]{1,0:T(8,128)} %get-tuple-element.5, f32[56,8,64,128]{3,2,1,0:T(8,128)S(1)} %bitcast.68), kind=kLoop, calls=%fused_computation.5 | loop fusion | flops 11010048 | bytes 44040192 | tf_op jit(solution)/shard_map/convert_element_type | solution.py:30
  291.0 4.1 copy.69
  295.2 6.0 %all-to-all-start.1 = ((bf16[448,8,1024]{2,0,1:T(8,128)(2,1)}), bf16[448,8,1024]{2,0,1:T(8,128)(2,1)}, u32[]{:S(2)}, u32[]{:S(2)}) async-start(bf16[448,8,1024]{2,0,1:T(8,128)(2,1)} %bitcast.69), calls=%async_computation.1 | async-start | bytes 14680064 | tf_op jit(solution)/shard_map/all_to_all | solution.py:65
  301.2 16.1 %copy.52 = bf16[448,8,2,1024]{3,1,2,0:T(8,128)(2,1)} copy(bf16[448,8,2,1024]{3,2,1,0:T(2,128)(2,1)} %bitcast.71) | data formatting | bytes 29360128
  317.3 7.2 %fusion.57 = f32[16,2048]{1,0:T(8,128)S(1)} fusion(bf16[16,3584]{1,0:T(8,128)(2,1)S(1)} %reshape.99, bf16[3584,2048]{1,0:T(8,128)(2,1)} %bitcast.66), kind=kOutput, calls=%fused_computation.57 | convolution fusion | flops 234881024 | bytes 14925824 | tf_op jit(solution)/shard_map/dot_general | solution.py:38
  324.6 137.1 %all-to-all-done.1 = bf16[448,8,1024]{2,0,1:T(8,128)(2,1)} async-done(((bf16[448,8,1024]{2,0,1:T(8,128)(2,1)}), bf16[448,8,1024]{2,0,1:T(8,128)(2,1)}, u32[]{:S(2)}, u32[]{:S(2)}) %all-to-all-start.1) | async-done | bytes 7340064 | tf_op jit(solution)/shard_map/all_to_all | solution.py:65
  461.7 5.0 %copy.51 = bf16[448,8,8,128]{3,2,1,0:T(8,128)(2,1)S(1)} copy(bf16[448,8,8,128]{3,1,2,0:T(8,128)(2,1)} %bitcast.23) | data formatting | bytes 14680064
  466.7 2.1 fusion.12
  468.8 0.7 reshape.102
  469.5 3.6 all-to-all-start.3
  473.2 7.1 %all-to-all-done.3 = bf16[8,2,3584]{2,1,0:T(2,128)(2,1)S(1)} async-done(((bf16[8,2,3584]{2,1,0:T(2,128)(2,1)}), bf16[8,2,3584]{2,1,0:T(2,128)(2,1)S(1)}, u32[]{:S(2)}, u32[]{:S(2)}) %all-to-all-start.3) | async-done | bytes 114720 | tf_op jit(solution)/shard_map/all_to_all | solution.py:101
  480.3 0.9 fusion.11
  (21 shorter events, 1.1 us)
Async XLA Ops:
  7.2 1.7 copy-start
  7.2 183.1 %all-gather.2.cloned.1.call-start = ((), (), s32[]{:S(2)}) async-start(), calls=%async_computation.4 | async-start | bytes 36700160 | tf_op jit(solution)/shard_map/all_gather | solution.py:58
  10.0 252.9 %all-to-all-start.2 = ((bf16[8,2,3584]{2,1,0:T(2,128)(2,1)}), bf16[8,2,3584]{2,1,0:T(2,128)(2,1)S(1)}, u32[]{:S(2)}, u32[]{:S(2)}) async-start(bf16[8,2,3584]{2,1,0:T(2,128)(2,1)} %copy.32), calls=%async_computation.2 | async-start | bytes 229376 | tf_op jit(solution)/shard_map/all_to_all | solution.py:95
  262.9 32.3 %all-to-all-start = ((bf16[448,8,8]{0,2,1:T(8,128)(2,1)}), bf16[448,8,8]{0,2,1:T(8,128)(2,1)S(1)}, u32[]{:S(2)}, u32[]{:S(2)}) async-start(bf16[448,8,8]{0,2,1:T(8,128)(2,1)} %get-tuple-element.10), calls=%async_computation | async-start | bytes 131072 | tf_op jit(solution)/shard_map/all_to_all | solution.py:66
  295.2 166.6 %all-to-all-start.1 = ((bf16[448,8,1024]{2,0,1:T(8,128)(2,1)}), bf16[448,8,1024]{2,0,1:T(8,128)(2,1)}, u32[]{:S(2)}, u32[]{:S(2)}) async-start(bf16[448,8,1024]{2,0,1:T(8,128)(2,1)} %bitcast.69), calls=%async_computation.1 | async-start | bytes 14680064 | tf_op jit(solution)/shard_map/all_to_all | solution.py:65
  317.3 164.0 %copy-start.1 = (bf16[2,3584]{1,0:T(2,128)(2,1)S(1)}, bf16[2,3584]{1,0:T(2,128)(2,1)}, u32[]{:S(2)}) copy-start(bf16[2,3584]{1,0:T(2,128)(2,1)} %param.13) | copy-start | bytes 43012
  324.5 148.6 %copy-start.2 = (bf16[2,4]{1,0:T(2,128)(2,1)S(1)}, bf16[2,4]{1,0:T(2,128)(2,1)}, u32[]{:S(2)}) copy-start(bf16[2,4]{1,0:T(2,128)(2,1)} %param.15) | copy-start | bytes 52
  469.5 10.9 %all-to-all-start.3 = ((bf16[8,2,3584]{2,1,0:T(2,128)(2,1)}), bf16[8,2,3584]{2,1,0:T(2,128)(2,1)S(1)}, u32[]{:S(2)}, u32[]{:S(2)}) async-start(bf16[8,2,3584]{2,1,0:T(2,128)(2,1)} %reshape.102), calls=%async_computation.3 | async-start | bytes 229376 | tf_op jit(solution)/shard_map/all_to_all | solution.py:101
Sparse Core Ops, SparseCore 0:
  9.6 180.6 all-gather.1
